TPU v7x, 32 devices: a whole 2x2x4 slice. The times are simulated.
32 devices in a mesh: attn: 8 (over z, x), expert: 4 (over y, core).
Axes of the slice: x: 2, y: 2, z: 4, core: 2. Of those that a mesh axis runs over, the one named last changes fastest.
Arguments:
- resid: bfloat16 [512, 6144], P('attn', 'expert')
- query: bfloat16 [512, 6144], P('attn', 'expert'), may hold values from -1 to 1
- key_cache: bfloat16 [512, 8, 128, 128], P('attn', 'expert'), may hold values from -4 to 4
- value_cache: bfloat16 [512, 8, 128, 128], P('attn', 'expert'), may hold values from -6 to 6
- new_key: bfloat16 [512, 1024], P('attn', 'expert'), may hold values from -4 to 4
- new_value: bfloat16 [512, 1024], P('attn', 'expert'), may hold values from -6 to 6
- lengths: int32 [512], P('attn'), may hold values from 1 to 128, as said below
- norm_gain: float32 [6144], P('expert'), may hold values from 0.1 to 1.9
- router_weight: float32 [6144, 8], P('expert'), may hold values from -0.078125 to 0.078125
- expert_ids: int32 [512, 2], P('attn'), may hold values from 0 to 7, as said below
- w_gate: bfloat16 [8, 6144, 8192], P('expert', None, 'attn'), may hold values from -0.078125 to 0.078125
- w_up: bfloat16 [8, 6144, 8192], P('expert', None, 'attn'), may hold values from -0.078125 to 0.078125
- w_down: bfloat16 [8, 8192, 6144], P('expert', 'attn'), may hold values from -0.0625 to 0.0625
Outputs:
- layer_out: bfloat16 [512, 6144], P('attn', 'expert')
Inputs may be any that keep to these rules, and one draw needn't show every extreme that they name: `expert_ids`: each row names two different experts. Within each aligned block of 64 rows (the rows of one index of attn) no expert is named by more than 32 rows, and one expert, the same in every block, is named by exactly 32 rows in each block. `lengths`: some row has all 128 positions filled and some row has one.
All inputs are finite; a program needn't handle non-finite values.
Results may differ from a plain program's by a relative error of at most 0.0095.
Values may be sent and summed in bfloat16 or wider, within the bound.
A program may use at most 128 MiB of HBM per device.

v0:
```python
import math
import jax
import jax.numpy as jnp
from jax import lax
from jax.sharding import PartitionSpec as P

D = 6144
E = 8
CAP = 32
EPSILON = 1e-05


def on_device(
    resid,
    query,
    key_cache,
    value_cache,
    new_key,
    new_value,
    lengths,
    norm_gain,
    router_weight,
    expert_ids,
    w_gate,
    w_up,
    w_down,
):
    row_count = resid.shape[0]
    width_local = resid.shape[1]
    kv_local = key_cache.shape[1]
    cache_slots = key_cache.shape[2]
    head_size = key_cache.shape[3]
    group_size = query.shape[1] // (kv_local * head_size)
    local_experts = w_gate.shape[0]
    expert_devices = lax.axis_size("expert")
    score_scale = 1.0 / math.sqrt(head_size)
    queries = query.reshape(row_count, kv_local, group_size, head_size)
    scores = (
        jnp.einsum("rkgd,rkld->rkgl", queries, key_cache, preferred_element_type=jnp.float32)
        * score_scale
    )
    fresh_score = (
        jnp.einsum(
            "rkgd,rkd->rkg",
            queries,
            new_key.reshape(row_count, kv_local, head_size),
            preferred_element_type=jnp.float32,
        )
        * score_scale
    )
    usable = lax.broadcasted_iota(jnp.int32, (row_count, cache_slots), 1) < lengths[:, None]
    powers = jnp.where(usable[:, None, None, :], jnp.exp(scores), jnp.float32(0.0))
    fresh_power = jnp.exp(fresh_score)
    denominator = jnp.sum(powers, axis=-1) + fresh_power
    weights_cache = (powers / denominator[..., None]).astype(jnp.bfloat16)
    weight_fresh = (fresh_power / denominator).astype(jnp.bfloat16)
    attended = jnp.einsum(
        "rkgl,rkld->rkgd", weights_cache, value_cache, preferred_element_type=jnp.float32
    )
    attended = attended + weight_fresh.astype(jnp.float32)[..., None] * new_value.astype(
        jnp.float32
    ).reshape(row_count, kv_local, 1, head_size)
    hidden_state = resid.astype(jnp.float32) + attended.reshape(row_count, width_local)
    total_square = lax.psum(jnp.sum(hidden_state * hidden_state, axis=1), "expert")
    normed = hidden_state * lax.rsqrt(total_square / D + EPSILON)[:, None] * norm_gain
    logits = lax.psum(jnp.dot(normed, router_weight, precision=lax.Precision.HIGHEST), "expert")
    narrow = normed.astype(jnp.bfloat16)
    choose = expert_ids[:, :, None] == lax.broadcasted_iota(jnp.int32, (1, 1, E), 2)
    picked = jnp.sum(jnp.where(choose, logits[:, None, :], jnp.float32(0.0)), axis=2)
    first_weight = 1.0 / (1.0 + jnp.exp(picked[:, 1] - picked[:, 0]))
    second_weight = 1.0 / (1.0 + jnp.exp(picked[:, 0] - picked[:, 1]))
    hits = jnp.sum(choose.astype(jnp.int32), axis=1)
    before = jnp.cumsum(hits, axis=0) - hits
    slot_index = jnp.sum(jnp.where(choose, before[:, None, :], 0), axis=2)
    slot_match = slot_index[:, :, None] == lax.broadcasted_iota(jnp.int32, (1, 1, CAP), 2)
    selector = jnp.einsum(
        "rke,rkc->ecr",
        choose.astype(jnp.bfloat16),
        slot_match.astype(jnp.bfloat16),
        preferred_element_type=jnp.float32,
    ).astype(jnp.bfloat16)
    whole_rows = lax.all_gather(narrow, "expert", axis=1, tiled=True)
    own_selector = lax.dynamic_slice_in_dim(
        selector, lax.axis_index("expert") * local_experts, local_experts, 0
    )
    outgoing = jnp.einsum(
        "ecr,rd->ecd", own_selector, whole_rows, preferred_element_type=jnp.float32
    ).astype(jnp.bfloat16)
    slab_rows = lax.all_gather(outgoing, "attn", axis=1, tiled=True)
    gate_part = jnp.einsum("end,edf->enf", slab_rows, w_gate, preferred_element_type=jnp.float32)
    up_part = jnp.einsum("end,edf->enf", slab_rows, w_up, preferred_element_type=jnp.float32)
    activation = (jax.nn.silu(gate_part) * up_part).astype(jnp.bfloat16)
    summed = lax.psum_scatter(
        jnp.einsum("enf,efd->ned", activation, w_down, preferred_element_type=jnp.float32).astype(
            jnp.bfloat16
        ),
        "attn",
        scatter_dimension=0,
        tiled=True,
    )
    expert_result = summed
    expert_result = expert_result.reshape(CAP, local_experts, expert_devices, width_local)
    returned = lax.all_to_all(expert_result, "expert", split_axis=2, concat_axis=1, tiled=True)
    flat_result = returned.reshape(CAP * E, width_local)
    target_index = slot_index * E + expert_ids
    picker = (
        target_index[:, :, None] == lax.broadcasted_iota(jnp.int32, (1, 1, CAP * E), 2)
    ).astype(jnp.bfloat16)
    taken = jnp.einsum("rkm,md->krd", picker, flat_result, preferred_element_type=jnp.float32)
    total = hidden_state + first_weight[:, None] * taken[0] + second_weight[:, None] * taken[1]
    return total.astype(jnp.bfloat16)


def solution(mesh):
    return jax.shard_map(
        on_device,
        mesh=mesh,
        in_specs=(
            P("attn", "expert"),
            P("attn", "expert"),
            P("attn", "expert", None, None),
            P("attn", "expert", None, None),
            P("attn", "expert"),
            P("attn", "expert"),
            P("attn"),
            P("expert"),
            P("expert", None),
            P("attn", None),
            P("expert", None, "attn"),
            P("expert", None, "attn"),
            P("expert", "attn", None),
        ),
        out_specs=P("attn", "expert"),
        check_vma=False,
    )
```

profile of v0, /device:TPU:0, one launch (start us, length us, event | category | flops | bytes accessed | tf_op | source)
XLA Modules:
  0.0 324.4 jit_solution(12968321372887208241)
XLA Ops:
  6.5 0.7 iota_compare_fusion.4
  7.3 0.8 copy.40
  8.3 1.2 select_reduce_fusion
  9.6 0.8 reshape.61
  10.4 0.8 reshape.55
  11.2 0.4 fusion.14
  11.6 1.2 reshape.50
  13.0 4.6 %fusion.25 = (f32[64,2,6]{2,1,0:T(2,128)S(1)}, f32[64,2,6,128]{3,2,1,0:T(8,128)S(1)}) fusion(bf16[64,2,6,128]{3,2,1,0:T(8,128)(2,1)S(1)} %reshape.50, bf16[64,2,128,128]{3,2,1,0:T(8,128)(2,1)} %param.15, pred[64,128]{1,0:T(8,128)(4,1)S(1)} %iota_compare_fusion.4), kind=kOutput, calls=%fused_computation.51 | convolution fusion | flops 25459968 | bytes 4795392 | tf_op jit(solution)/shard_map/rkgd,rkld->rkgl/dot_general | solution.py:39
  17.8 3.4 %convolution_add_fusion = f32[64,2,6,128]{3,2,1,0:T(8,128)S(1)} fusion(bf16[64,2,128,128]{3,2,1,0:T(8,128)(2,1)} %param.16, f32[64,2,6,128]{3,2,1,0:T(8,128)S(1)} %get-tuple-element.12, f32[64,2,128]{2,1,0:T(2,128)S(1)} %reshape.55, f32[64,2,6]{2,1,0:T(2,128)S(1)} %get-tuple-element.6, f32[64,2,6]{2,1,0:T(2,128)S(1)} %get-tuple-element.5), kind=kOutput, calls=%fused_computation.5 | convolution fusion | flops 25559040 | bytes 5052416 | tf_op jit(solution)/shard_map/rkgl,rkld->rkgd/dot_general | solution.py:57
  21.5 8.4 %psum.14 = f32[64]{0:T(128)S(1)} all-reduce(f32[64]{0:T(128)S(1)} %multiply_reduce_fusion), channel_id=1, replica_groups=mesh['attn'=8,'expert'=4] {'expert'}, use_global_device_ids=true, to_apply=%region_2.3 | all-reduce | flops 64 | bytes 512 | tf_op jit(solution)/shard_map/psum | solution.py:64
  30.0 7.5 %all_gather.6 = bf16[64,6144]{1,0:T(8,128)(2,1)S(1)} all-gather(bf16[64,1536]{1,0:T(8,128)(2,1)S(1)} %fusion.9), channel_id=1, replica_groups=mesh['attn'=8,'expert'=4] {'expert'}, dimensions={1}, use_global_device_ids=true | all-gather | bytes 983040 | tf_op jit(solution)/shard_map/all_gather | solution.py:82
  37.5 1.3 convolution_convert_fusion.1
  39.1 100.0 %all-gather.2.cloned.1.call-done = bf16[2,256,6144]{2,1,0:T(8,128)(2,1)} async-done(((bf16[2,32,6144]{2,1,0:T(8,128)(2,1)}), bf16[2,256,6144]{2,1,0:T(8,128)(2,1)}) %all-gather.2.cloned.1.call-update) | async-done | bytes 6291472 | tf_op jit(solution)/shard_map/all_gather | solution.py:89
  139.1 13.5 %fusion.27 = f32[2,256,1024]{2,1,0:T(8,128)S(1)} fusion(bf16[2,256,6144]{2,1,0:T(8,128)(2,1)} %all-gather.2.cloned.1.call-done, bf16[2,6144,1024]{2,1,0:T(8,128)(2,1)} %param.23), kind=kOutput, calls=%fused_computation.53 | convolution fusion | flops 6442450944 | bytes 33554432 | tf_op jit(solution)/shard_map/end,edf->enf/dot_general | solution.py:90
  152.6 12.3 %multiply_convert_fusion = bf16[2,256,1024]{2,1,0:T(8,128)(2,1)S(1)} fusion(f32[2,256,1024]{2,1,0:T(8,128)S(1)} %fusion.27, bf16[2,256,6144]{2,1,0:T(8,128)(2,1)S(1)} %copy-done.4, bf16[2,6144,1024]{2,1,0:T(8,128)(2,1)} %param.24), kind=kOutput, calls=%fused_computation.4 | convolution fusion | flops 6445596672 | bytes 34603008 | tf_op jit(solution)/shard_map/end,edf->enf/dot_general | solution.py:91
  164.9 16.8 %fusion = bf16[256,2,6144]{2,0,1:T(8,128)(2,1)} fusion(bf16[2,256,1024]{2,1,0:T(8,128)(2,1)S(1)} %multiply_convert_fusion, bf16[2,1024,6144]{2,1,0:T(8,128)(2,1)} %param.25), kind=kOutput, calls=%fused_computation.1 | convolution fusion | flops 6445596672 | bytes 32505856 | tf_op jit(solution)/shard_map/enf,efd->ned/dot_general | solution.py:94
  181.8 0.5 fusion.10
  182.3 5.7 %psum.15 = f32[64,8]{0,1:T(8,128)S(1)} all-reduce(f32[64,8]{0,1:T(8,128)S(1)} %fusion.10), channel_id=1, replica_groups=mesh['attn'=8,'expert'=4] {'expert'}, use_global_device_ids=true, to_apply=%region_3.4 | all-reduce | flops 512 | bytes 4096 | tf_op jit(solution)/shard_map/psum | solution.py:66
  188.3 109.8 %reduce-scatter.2.cloned.1.call-done = bf16[32,2,6144]{2,0,1:T(8,128)(2,1)} async-done(((bf16[256,2,6144]{2,0,1:T(8,128)(2,1)}), bf16[32,2,6144]{2,0,1:T(8,128)(2,1)}) %reduce-scatter.2.cloned.1.call-update) | async-done | bytes 786448 | tf_op jit(solution)/shard_map/reduce_scatter | solution.py:93
  298.1 2.1 copy.56
  300.2 3.5 %all-to-all-start = ((bf16[32,2,4,1536]{3,0,1,2:T(8,128)(2,1)}), bf16[32,2,4,1536]{3,0,1,2:T(8,128)(2,1)S(1)}, u32[]{:S(2)}, u32[]{:S(2)}) async-start(bf16[32,2,4,1536]{3,0,1,2:T(8,128)(2,1)} %bitcast.52), calls=%async_computation.1 | async-start | bytes 1572864 | tf_op jit(solution)/shard_map/all_to_all | solution.py:103
  304.0 11.3 %all-to-all-done = bf16[32,2,4,1536]{3,0,1,2:T(8,128)(2,1)S(1)} async-done(((bf16[32,2,4,1536]{3,0,1,2:T(8,128)(2,1)}), bf16[32,2,4,1536]{3,0,1,2:T(8,128)(2,1)S(1)}, u32[]{:S(2)}, u32[]{:S(2)}) %all-to-all-start) | async-done | bytes 786464 | tf_op jit(solution)/shard_map/all_to_all | solution.py:103
  315.3 0.8 copy.46
  316.7 0.8 fusion.6
  (34 shorter events, 2.5 us)
Async XLA Ops:
  6.5 175.3 %copy-start = (f32[1536,8]{0,1:T(8,128)S(1)}, f32[1536,8]{0,1:T(8,128)}, u32[]{:S(2)}) copy-start(f32[1536,8]{0,1:T(8,128)} %param.21) | copy-start | bytes 147460
  6.5 132.5 %all-gather.2.cloned.1.call-start = ((), (), s32[]{:S(2)}) async-start(), calls=%async_computation.2 | async-start | bytes 7077888 | tf_op jit(solution)/shard_map/all_gather | solution.py:89
  13.0 8.3 %copy-start.1 = (bf16[64,1536]{1,0:T(8,128)(2,1)S(1)}, bf16[64,1536]{1,0:T(8,128)(2,1)}, u32[]{:S(2)}) copy-start(bf16[64,1536]{1,0:T(8,128)(2,1)} %param.13) | copy-start | bytes 589828
  17.7 12.2 %copy-start.2 = (f32[1536]{0:T(1024)S(1)}, f32[1536]{0:T(1024)}, u32[]{:S(2)}) copy-start(f32[1536]{0:T(1024)} %param.20) | copy-start | bytes 18436
  38.8 259.3 %reduce-scatter.2.cloned.1.call-start = ((), (), s32[]{:S(2)}) async-start(), calls=%async_computation.3 | async-start | bytes 7077888 | tf_op jit(solution)/shard_map/reduce_scatter | solution.py:93
  139.1 13.6 %copy-start.4 = (bf16[2,256,6144]{2,1,0:T(8,128)(2,1)S(1)}, bf16[2,256,6144]{2,1,0:T(8,128)(2,1)}, u32[]{:S(2)}) copy-start(bf16[2,256,6144]{2,1,0:T(8,128)(2,1)} %all-gather.2.cloned.1.call-done) | copy-start | bytes 18874372
  181.7 122.2 %copy-start.3 = (s32[64,2]{0,1:T(2,128)S(1)}, s32[64,2]{0,1:T(2,128)}, u32[]{:S(2)}) copy-start(s32[64,2]{0,1:T(2,128)} %param.22) | copy-start | bytes 1540
  300.2 15.1 %all-to-all-start = ((bf16[32,2,4,1536]{3,0,1,2:T(8,128)(2,1)}), bf16[32,2,4,1536]{3,0,1,2:T(8,128)(2,1)S(1)}, u32[]{:S(2)}, u32[]{:S(2)}) async-start(bf16[32,2,4,1536]{3,0,1,2:T(8,128)(2,1)} %bitcast.52), calls=%async_computation.1 | async-start | bytes 1572864 | tf_op jit(solution)/shard_map/all_to_all | solution.py:103
Sparse Core Ops, SparseCore 0:
  39.0 100.0 all-gather.1
  181.9 116.1 reduce-scatter.1
where the time goes:
time: 325 us; the launch traced here: 324 us
  waiting for transfers between devices  221 us (68%)
  matrix products  53.5 us (16%)
  blocking collectives  21.5 us (7%)
  between operations  13.6 us (4%)
  local copies, waits for them, and re-layouts  7.22 us (2%)
  starting transfers between devices  3.72 us (1%)
  other arithmetic  3.66 us (1%)
    reduce_scatter x1, waiting for transfers between devices, on_device(): lax.psum_scatter(jnp.einsum('enf,efd->ned', activation, w_down, preferred...  110 us
    all_gather x1, waiting for transfers between devices, on_device(): slab_rows = lax.all_gather(outgoing, 'attn', axis=1, tiled=True)  100 us
    dot_general x1, matrix products, on_device(): jnp.einsum('enf,efd->ned', activation, w_down, preferred_element_type=jnp...  16.8 us
    dot_general x1, matrix products, on_device(): jnp.einsum('end,edf->enf', slab_rows, w_gate, preferred_element_type=jnp....  13.5 us
    dot_general x1, matrix products, on_device(): jnp.einsum('end,edf->enf', slab_rows, w_up, preferred_element_type=jnp.fl...  12.3 us
    all_to_all x1, waiting for transfers between devices, on_device(): lax.all_to_all(expert_result, 'expert', split_axis=2, concat_axis=1, tile...  11.3 us
    psum x1, blocking collectives, on_device(): lax.psum(jnp.sum(hidden_state * hidden_state, axis=1), 'expert')  8.4 us
    all_gather x1, blocking collectives, on_device(): whole_rows = lax.all_gather(narrow, 'expert', axis=1, tiled=True)  7.47 us
  transfers between devices with their start and end apart: 3, of which 3 were waited for; matrix products, arithmetic and copies ran while one was open for 0% of the time, Pallas kernels for 0%

commit v1 on v0

--- a/solution.py
+++ b/solution.py
@@ -86,7 +86,12 @@
     outgoing = jnp.einsum(
         "ecr,rd->ecd", own_selector, whole_rows, preferred_element_type=jnp.float32
     ).astype(jnp.bfloat16)
-    slab_rows = lax.all_gather(outgoing, "attn", axis=1, tiled=True)
+    ring = [outgoing]
+    for hop in range(7):
+        ring.append(lax.ppermute(ring[-1], "attn", [(dev, (dev + 1) % 8) for dev in range(8)]))
+    slab_rows = jnp.roll(
+        jnp.concatenate(ring[::-1], axis=1), (lax.axis_index("attn") + 1) * ring[0].shape[1], axis=1
+    )
     gate_part = jnp.einsum("end,edf->enf", slab_rows, w_gate, preferred_element_type=jnp.float32)
     up_part = jnp.einsum("end,edf->enf", slab_rows, w_up, preferred_element_type=jnp.float32)
     activation = (jax.nn.silu(gate_part) * up_part).astype(jnp.bfloat16)

time: 325 us -> 389 us (1.20)
  waiting for transfers between devices: 221 us -> 259 us
  local copies, waits for them, and re-layouts: 7.22 us -> 33.2 us
    ppermute x0 -> x7, waiting for transfers between devices: none -> 140 us  [on_device(): lax.ppermute(ring[-1], 'attn', [(dev, (dev + 1) % 8) for dev in range(8)])]
    all_gather x1 -> x0, waiting for transfers between devices: 100 us -> none  [on_device(): slab_rows = lax.all_gather(outgoing, 'attn', axis=1, tiled=True)]
    unnamed x13 -> x38, local copies, waits for them, and re-layouts: 0.94 us -> 25.9 us
  transfers between devices with their start and end apart: 3 -> 9, of which waited for: 3 -> 9; matrix products, arithmetic and copies ran while one was open for 0% -> 0% of each run, Pallas kernels for 0% -> 0%
where the time goes in v1:
time: 389 us; the launch traced here: 388 us
  waiting for transfers between devices  259 us (67%)
  matrix products  51.9 us (13%)
  local copies, waits for them, and re-layouts  33.2 us (9%)
  blocking collectives  21.5 us (6%)
  between operations  13.6 us (3%)
  starting transfers between devices  5.16 us (1%)
    ppermute x7, waiting for transfers between devices, on_device(): lax.ppermute(ring[-1], 'attn', [(dev, (dev + 1) % 8) for dev in range(8)])  140 us
    reduce_scatter x1, waiting for transfers between devices, on_device(): lax.psum_scatter(jnp.einsum('enf,efd->ned', activation, w_down, preferred...  108 us
    unnamed x38, local copies, waits for them, and re-layouts  25.9 us
    dot_general x1, matrix products, on_device(): jnp.einsum('end,edf->enf', slab_rows, w_gate, preferred_element_type=jnp....  14.4 us
    dot_general x1, matrix products, on_device(): jnp.einsum('enf,efd->ned', activation, w_down, preferred_element_type=jnp...  14.2 us
    dot_general x1, matrix products, on_device(): jnp.einsum('end,edf->enf', slab_rows, w_up, preferred_element_type=jnp.fl...  13.4 us
    all_to_all x1, waiting for transfers between devices, on_device(): lax.all_to_all(expert_result, 'expert', split_axis=2, concat_axis=1, tile...  11.3 us
    psum x1, blocking collectives, on_device(): lax.psum(jnp.sum(hidden_state * hidden_state, axis=1), 'expert')  8.39 us
  transfers between devices with their start and end apart: 9, of which 9 were waited for; matrix products, arithmetic and copies ran while one was open for 0% of the time, Pallas kernels for 0%

profile of v1, /device:TPU:0, one launch (start us, length us, event | category | flops | bytes accessed | tf_op | source)
XLA Modules:
  0.0 388.5 jit_solution(13765366494127515346)
XLA Ops:
  13.1 4.6 %fusion.33 = (f32[64,2,6]{2,1,0:T(2,128)S(1)}, f32[64,2,6,128]{3,2,1,0:T(8,128)S(1)}) fusion(bf16[64,2,6,128]{3,2,1,0:T(8,128)(2,1)S(1)} %reshape.50, bf16[64,2,128,128]{3,2,1,0:T(8,128)(2,1)} %param.15, pred[64,128]{1,0:T(8,128)(4,1)S(1)} %iota_compare_fusion.4), kind=kOutput, calls=%fused_computation.75 | convolution fusion | flops 25459968 | bytes 4795392 | tf_op jit(solution)/shard_map/rkgd,rkld->rkgl/dot_general | solution.py:39
  17.8 3.4 convolution_add_fusion
  21.5 8.4 %psum.14 = f32[64]{0:T(128)S(1)} all-reduce(f32[64]{0:T(128)S(1)} %multiply_reduce_fusion), channel_id=1, replica_groups=mesh['attn'=8,'expert'=4] {'expert'}, use_global_device_ids=true, to_apply=%region_2.3 | all-reduce | flops 64 | bytes 512 | tf_op jit(solution)/shard_map/psum | solution.py:64
  30.0 7.5 %all_gather.3 = bf16[64,6144]{1,0:T(8,128)(2,1)S(1)} all-gather(bf16[64,1536]{1,0:T(8,128)(2,1)S(1)} %fusion.14), channel_id=1, replica_groups=mesh['attn'=8,'expert'=4] {'expert'}, dimensions={1}, use_global_device_ids=true | all-gather | bytes 983040 | tf_op jit(solution)/shard_map/all_gather | solution.py:82
  39.5 21.1 %collective-permute-done = bf16[2,32,6144]{2,1,0:T(8,128)(2,1)S(1)} collective-permute-done((bf16[2,32,6144]{2,1,0:T(8,128)(2,1)S(1)}, bf16[2,32,6144]{2,1,0:T(8,128)(2,1)S(1)}, u32[]{:S(2)}, u32[]{:S(2)}) %collective-permute-start) | collective-permute-done | bytes 786464 | tf_op jit(solution)/shard_map/ppermute | solution.py:91
  60.7 21.8 %collective-permute-done.1 = bf16[2,32,6144]{2,1,0:T(8,128)(2,1)S(1)} collective-permute-done((bf16[2,32,6144]{2,1,0:T(8,128)(2,1)S(1)}, bf16[2,32,6144]{2,1,0:T(8,128)(2,1)S(1)}, u32[]{:S(2)}, u32[]{:S(2)}) %collective-permute-start.1) | collective-permute-done | bytes 786464 | tf_op jit(solution)/shard_map/ppermute | solution.py:91
  82.5 21.0 %collective-permute-done.2 = bf16[2,32,6144]{2,1,0:T(8,128)(2,1)S(1)} collective-permute-done((bf16[2,32,6144]{2,1,0:T(8,128)(2,1)S(1)}, bf16[2,32,6144]{2,1,0:T(8,128)(2,1)S(1)}, u32[]{:S(2)}, u32[]{:S(2)}) %collective-permute-start.2) | collective-permute-done | bytes 786464 | tf_op jit(solution)/shard_map/ppermute | solution.py:91
  104.4 20.1 %collective-permute-done.3 = bf16[2,32,6144]{2,1,0:T(8,128)(2,1)S(1)} collective-permute-done((bf16[2,32,6144]{2,1,0:T(8,128)(2,1)S(1)}, bf16[2,32,6144]{2,1,0:T(8,128)(2,1)S(1)}, u32[]{:S(2)}, u32[]{:S(2)}) %collective-permute-start.3) | collective-permute-done | bytes 786464 | tf_op jit(solution)/shard_map/ppermute | solution.py:91
  125.4 19.3 %collective-permute-done.4 = bf16[2,32,6144]{2,1,0:T(8,128)(2,1)S(1)} collective-permute-done((bf16[2,32,6144]{2,1,0:T(8,128)(2,1)S(1)}, bf16[2,32,6144]{2,1,0:T(8,128)(2,1)S(1)}, u32[]{:S(2)}, u32[]{:S(2)}) %collective-permute-start.4) | collective-permute-done | bytes 786464 | tf_op jit(solution)/shard_map/ppermute | solution.py:91
  145.6 18.5 %collective-permute-done.5 = bf16[2,32,6144]{2,1,0:T(8,128)(2,1)} collective-permute-done((bf16[2,32,6144]{2,1,0:T(8,128)(2,1)S(1)}, bf16[2,32,6144]{2,1,0:T(8,128)(2,1)}, u32[]{:S(2)}, u32[]{:S(2)}) %collective-permute-start.5) | collective-permute-done | bytes 786464 | tf_op jit(solution)/shard_map/ppermute | solution.py:91
  164.1 17.9 %collective-permute-done.6 = bf16[2,32,6144]{2,1,0:T(8,128)(2,1)} collective-permute-done((bf16[2,32,6144]{2,1,0:T(8,128)(2,1)}, bf16[2,32,6144]{2,1,0:T(8,128)(2,1)}, u32[]{:S(2)}, u32[]{:S(2)}) %collective-permute-start.6) | collective-permute-done | bytes 786464 | tf_op jit(solution)/shard_map/ppermute | solution.py:91
  182.0 2.1 constant_dynamic-update-slice_fusion.15
  188.2 2.1 constant_dynamic-update-slice_fusion.12
  190.3 2.1 constant_dynamic-update-slice_fusion.11
  195.3 2.1 constant_dynamic-update-slice_fusion.7
  197.4 2.1 constant_dynamic-update-slice_fusion.6
  205.3 13.4 %fusion.1 = f32[2,256,1024]{2,1,0:T(8,128)S(1)} fusion(bf16[2,6144,1024]{2,1,0:T(8,128)(2,1)} %param.24, bf16[2,512,6144]{2,1,0:T(8,128)(2,1)} %constant_dynamic-update-slice_fusion, s32[]{:T(128)S(6)} %select_n.33), kind=kOutput, calls=%fused_computation.3 | convolution fusion | flops 6442450944 | bytes 33554436 | tf_op jit(solution)/shard_map/end,edf->enf/dot_general | solution.py:96
  218.7 14.4 %fusion.3 = f32[2,256,1024]{2,1,0:T(8,128)} fusion(bf16[2,6144,1024]{2,1,0:T(8,128)(2,1)} %param.23, bf16[2,512,6144]{2,1,0:T(8,128)(2,1)} %constant_dynamic-update-slice_fusion, s32[]{:T(128)S(6)} %select_n.33), kind=kOutput, calls=%fused_computation.5 | convolution fusion | flops 6442450944 | bytes 33554436 | tf_op jit(solution)/shard_map/end,edf->enf/dot_general | solution.py:95
  233.1 14.2 %fusion = bf16[256,2,6144]{2,0,1:T(8,128)(2,1)} fusion(bf16[2,1024,6144]{2,1,0:T(8,128)(2,1)} %param.25, f32[2,256,1024]{2,1,0:T(8,128)S(1)} %fusion.1, f32[2,256,1024]{2,1,0:T(8,128)} %fusion.3), kind=kOutput, calls=%fused_computation.1 | convolution fusion | flops 6448742400 | bytes 35651584 | tf_op jit(solution)/shard_map/enf,efd->ned/dot_general | solution.py:99
  247.9 5.7 %psum.15 = f32[64,8]{0,1:T(8,128)S(1)} all-reduce(f32[64,8]{0,1:T(8,128)S(1)} %fusion.15), channel_id=1, replica_groups=mesh['attn'=8,'expert'=4] {'expert'}, use_global_device_ids=true, to_apply=%region_3.4 | all-reduce | flops 512 | bytes 4096 | tf_op jit(solution)/shard_map/psum | solution.py:66
  253.9 108.3 %reduce-scatter.2.cloned.1.call-done = bf16[32,2,6144]{2,0,1:T(8,128)(2,1)} async-done(((bf16[256,2,6144]{2,0,1:T(8,128)(2,1)}), bf16[32,2,6144]{2,0,1:T(8,128)(2,1)}) %reduce-scatter.2.cloned.1.call-update) | async-done | bytes 786448 | tf_op jit(solution)/shard_map/reduce_scatter | solution.py:98
  362.2 2.1 copy.56
  364.3 3.5 all-to-all-start
  368.0 11.3 %all-to-all-done = bf16[32,2,4,1536]{3,0,1,2:T(8,128)(2,1)S(1)} async-done(((bf16[32,2,4,1536]{3,0,1,2:T(8,128)(2,1)}), bf16[32,2,4,1536]{3,0,1,2:T(8,128)(2,1)S(1)}, u32[]{:S(2)}, u32[]{:S(2)}) %all-to-all-start) | async-done | bytes 786464 | tf_op jit(solution)/shard_map/all_to_all | solution.py:108
  (71 shorter events, 27.9 us)
Async XLA Ops:
  6.5 240.9 %copy-start = (f32[1536,8]{0,1:T(8,128)S(1)}, f32[1536,8]{0,1:T(8,128)}, u32[]{:S(2)}) copy-start(f32[1536,8]{0,1:T(8,128)} %param.21) | copy-start | bytes 147460
  6.5 14.8 %copy-start.7 = (bf16[64,1536]{1,0:T(8,128)(2,1)S(1)}, bf16[64,1536]{1,0:T(8,128)(2,1)}, u32[]{:S(2)}) copy-start(bf16[64,1536]{1,0:T(8,128)(2,1)} %param.13) | copy-start | bytes 589828
  6.5 23.3 %copy-start.8 = (f32[1536]{0:T(1024)S(1)}, f32[1536]{0:T(1024)}, u32[]{:S(2)}) copy-start(f32[1536]{0:T(1024)} %param.20) | copy-start | bytes 18436
  6.5 355.7 %reduce-scatter.2.cloned.1.call-start = ((), (), s32[]{:S(2)}) async-start(), calls=%async_computation.2 | async-start | bytes 7077888 | tf_op jit(solution)/shard_map/reduce_scatter | solution.py:98
  37.9 22.8 %collective-permute-start = (bf16[2,32,6144]{2,1,0:T(8,128)(2,1)S(1)}, bf16[2,32,6144]{2,1,0:T(8,128)(2,1)S(1)}, u32[]{:S(2)}, u32[]{:S(2)}) collective-permute-start(bf16[2,32,6144]{2,1,0:T(8,128)(2,1)S(1)} %convolution_convert_fusion.1), channel_id=1, source_target_pairs={{0,4},{4,8},{8,12},{12,16},{16,20},{20,24},{24,28},{28,0},{1,5},{5... | collective-permute-start | bytes 2359304 | tf_op jit(solution)/shard_map/ppermute | solution.py:91
  60.6 21.8 %collective-permute-start.1 = (bf16[2,32,6144]{2,1,0:T(8,128)(2,1)S(1)}, bf16[2,32,6144]{2,1,0:T(8,128)(2,1)S(1)}, u32[]{:S(2)}, u32[]{:S(2)}) collective-permute-start(bf16[2,32,6144]{2,1,0:T(8,128)(2,1)S(1)} %collective-permute-done), channel_id=1, source_target_pairs={{0,4},{4,8},{8,12},{12,16},{16,20},{20,24},{24,28},{28,0},{1,5},{5... | collective-permute-start | bytes 2359304 | tf_op jit(solution)/shard_map/ppermute | solution.py:91
  82.5 21.0 %collective-permute-start.2 = (bf16[2,32,6144]{2,1,0:T(8,128)(2,1)S(1)}, bf16[2,32,6144]{2,1,0:T(8,128)(2,1)S(1)}, u32[]{:S(2)}, u32[]{:S(2)}) collective-permute-start(bf16[2,32,6144]{2,1,0:T(8,128)(2,1)S(1)} %collective-permute-done.1), channel_id=1, source_target_pairs={{0,4},{4,8},{8,12},{12,16},{16,20},{20,24},{24,28},{28,0},{1,5},{5... | collective-permute-start | bytes 2359304 | tf_op jit(solution)/shard_map/ppermute | solution.py:91
  103.5 0.9 copy-start.1
  104.4 20.1 %collective-permute-start.3 = (bf16[2,32,6144]{2,1,0:T(8,128)(2,1)S(1)}, bf16[2,32,6144]{2,1,0:T(8,128)(2,1)S(1)}, u32[]{:S(2)}, u32[]{:S(2)}) collective-permute-start(bf16[2,32,6144]{2,1,0:T(8,128)(2,1)S(1)} %collective-permute-done.2), channel_id=1, source_target_pairs={{0,4},{4,8},{8,12},{12,16},{16,20},{20,24},{24,28},{28,0},{1,5},{5... | collective-permute-start | bytes 2359304 | tf_op jit(solution)/shard_map/ppermute | solution.py:91
  124.5 0.9 copy-start.3
  125.4 19.3 %collective-permute-start.4 = (bf16[2,32,6144]{2,1,0:T(8,128)(2,1)S(1)}, bf16[2,32,6144]{2,1,0:T(8,128)(2,1)S(1)}, u32[]{:S(2)}, u32[]{:S(2)}) collective-permute-start(bf16[2,32,6144]{2,1,0:T(8,128)(2,1)S(1)} %collective-permute-done.3), channel_id=1, source_target_pairs={{0,4},{4,8},{8,12},{12,16},{16,20},{20,24},{24,28},{28,0},{1,5},{5... | collective-permute-start | bytes 2359304 | tf_op jit(solution)/shard_map/ppermute | solution.py:91
  144.7 0.9 copy-start.5
  145.6 18.5 %collective-permute-start.5 = (bf16[2,32,6144]{2,1,0:T(8,128)(2,1)S(1)}, bf16[2,32,6144]{2,1,0:T(8,128)(2,1)}, u32[]{:S(2)}, u32[]{:S(2)}) collective-permute-start(bf16[2,32,6144]{2,1,0:T(8,128)(2,1)S(1)} %collective-permute-done.4), channel_id=1, source_target_pairs={{0,4},{4,8},{8,12},{12,16},{16,20},{20,24},{24,28},{28,0},{1,5},{5... | collective-permute-start | bytes 2359304 | tf_op jit(solution)/shard_map/ppermute | solution.py:91
  164.1 17.9 %collective-permute-start.6 = (bf16[2,32,6144]{2,1,0:T(8,128)(2,1)}, bf16[2,32,6144]{2,1,0:T(8,128)(2,1)}, u32[]{:S(2)}, u32[]{:S(2)}) collective-permute-start(bf16[2,32,6144]{2,1,0:T(8,128)(2,1)} %collective-permute-done.5), channel_id=1, source_target_pairs={{0,4},{4,8},{8,12},{12,16},{16,20},{20,24},{24,28},{28,0},{1,5},{5... | collective-permute-start | bytes 2359304 | tf_op jit(solution)/shard_map/ppermute | solution.py:91
  164.1 35.4 %copy-start.6 = (bf16[2,32,6144]{2,1,0:T(8,128)(2,1)S(1)}, bf16[2,32,6144]{2,1,0:T(8,128)(2,1)}, u32[]{:S(2)}) copy-start(bf16[2,32,6144]{2,1,0:T(8,128)(2,1)} %copy-done.5) | copy-start | bytes 2359300
  164.1 36.3 %copy-start.4 = (bf16[2,32,6144]{2,1,0:T(8,128)(2,1)S(1)}, bf16[2,32,6144]{2,1,0:T(8,128)(2,1)}, u32[]{:S(2)}) copy-start(bf16[2,32,6144]{2,1,0:T(8,128)(2,1)} %copy-done.3) | copy-start | bytes 2359300
  164.1 37.3 %copy-start.2 = (bf16[2,32,6144]{2,1,0:T(8,128)(2,1)S(1)}, bf16[2,32,6144]{2,1,0:T(8,128)(2,1)}, u32[]{:S(2)}) copy-start(bf16[2,32,6144]{2,1,0:T(8,128)(2,1)} %copy-done.1) | copy-start | bytes 2359300
  233.1 134.9 %copy-start.9 = (s32[64,2]{0,1:T(2,128)S(1)}, s32[64,2]{0,1:T(2,128)}, u32[]{:S(2)}) copy-start(s32[64,2]{0,1:T(2,128)} %param.22) | copy-start | bytes 1540
  364.3 15.1 %all-to-all-start = ((bf16[32,2,4,1536]{3,0,1,2:T(8,128)(2,1)}), bf16[32,2,4,1536]{3,0,1,2:T(8,128)(2,1)S(1)}, u32[]{:S(2)}, u32[]{:S(2)}) async-start(bf16[32,2,4,1536]{3,0,1,2:T(8,128)(2,1)} %bitcast.49), calls=%async_computation.1 | async-start | bytes 1572864 | tf_op jit(solution)/shard_map/all_to_all | solution.py:108
Sparse Core Ops, SparseCore 0:
  247.4 114.7 reduce-scatter.1
